TPU v7x, 512 devices: a whole 4x8x8 slice. The times are simulated.
512 devices in a mesh: gx: 8 (over z), gy: 8 (over y_lo, core), gz: 8 (over y_hi, x).
Axes of the slice: x: 4, y: 8 (y_hi: 2, y_lo: 4; y = y_hi * 4 + y_lo), z: 8, core: 2. Of those that a mesh axis runs over, the one named last changes fastest.
Arguments:
- x_in: bfloat16 [3072, 5120], P(('gy', 'gx'), 'gz'), may hold values from -190 to 190
- gain: float32 [5120], P('gz'), may hold values from 0.25 to 1.75
- w_up: bfloat16 [5120, 7168], P(('gz', 'gy'), 'gx'), may hold values from -0.078125 to 0.078125
- w_down: bfloat16 [7168, 5120], P(('gx', 'gy'), 'gz'), may hold values from -0.0625 to 0.0625
- d_out: bfloat16 [3072, 5120], P(('gy', 'gx'), 'gz'), may hold values from -1.1953125 to 1.1953125
Outputs:
- d_x: bfloat16 [3072, 5120], P(('gy', 'gx'), 'gz')
- d_w_up: bfloat16 [5120, 7168], P(('gz', 'gy'), 'gx')
- d_w_down: bfloat16 [7168, 5120], P(('gx', 'gy'), 'gz')
- d_gain: float32 [5120], P('gz')
All inputs are finite; a program needn't handle non-finite values.
Results may differ from a plain program's by a relative error of at most 0.02.
Values may be sent and summed in bfloat16 or wider, within the bound.
No kernel may reach another device: no remote copies, remote signals or barrier semaphores. Data moves between devices by JAX's collectives and lax.ppermute only.
A program may use at most 64 MiB of HBM per device.

v0:
```python
import jax
import jax.numpy as jnp
from jax import lax
from jax.sharding import Mesh
from jax.sharding import PartitionSpec as P

BF, F32 = (jnp.bfloat16, jnp.float32)
LANES = 128
GY, GZ = (("yl", "co"), ("yh", "xx"))


def gelu_pair(hidden):
    cdf = 0.5 * (1.0 + jax.scipy.special.erf(hidden * 0.7071067811865476))
    slope = cdf + hidden * jnp.exp(-0.5 * hidden * hidden) * 0.3989422804014327
    return (hidden * cdf, slope)


def exchange(blocks, axis):
    return lax.all_to_all(blocks, axis, 0, 0, tiled=True)


def spread(value, axis):
    n = lax.axis_size(axis)
    return exchange(jnp.broadcast_to(value[None], (n, *value.shape)), axis)


def summed(blocks):
    return jnp.sum(blocks.astype(F32), axis=0)


def pieces(value):
    high = lax.reduce_precision(value, 8, 7)
    rest = value - high
    middle = lax.reduce_precision(rest, 8, 7)
    return [p.astype(BF) for p in (high, middle, rest - middle)]


def columns(*values):
    return jnp.stack([p for v in values for p in pieces(v)], axis=-1)


def column(lanes, index):
    return jnp.sum(lanes[..., 3 * index : 3 * index + 3].astype(F32), axis=-1)


def swap(value, axis, bits):
    return lax.ppermute(value, axis, [(i, i ^ bits) for i in range(lax.axis_size(axis))])


def other_core(value):
    return swap(value, "co", 1)


def dot(a, b, contract):
    return lax.dot_general(
        a, b, ((contract[:1], contract[1:]), ((), ())), preferred_element_type=F32
    )


def body(x_in, gain, w_up, w_down, d_out):
    rows, local = x_in.shape
    n_gx, n_yl, n_gz = (lax.axis_size(a) for a in ("gx", "yl", GZ))
    width = local * n_gz
    up_rows, hid = w_up.shape
    down_rows = w_down.shape[0]
    all_rows = rows * n_gx
    block = all_rows // n_gz
    even = lax.axis_index("co") == 0

    def by_core(mine, other):
        pair = [jnp.where(even, mine, other), jnp.where(even, other, mine)]
        return jnp.stack(pair, axis=1).reshape(-1, mine.shape[-1])

    down_full = lax.all_gather(w_down, GY, axis=0, tiled=True)
    up_mine = spread(w_up, "yl")
    both = lax.all_gather(jnp.concatenate([x_in, d_out], axis=1), "gx", axis=0, tiled=True)
    both, up_mine = lax.optimization_barrier((both, up_mine))
    up_full = by_core(up_mine, other_core(up_mine))
    x_rows, out_rows = (both[:, :local].astype(F32), both[:, local:])
    part_sum = jnp.sum(x_rows, axis=1)
    off = x_rows - (part_sum / local)[:, None]
    second = jnp.sum(off * off, axis=1)
    y = (off * gain).astype(BF)
    gains = jnp.pad(jnp.stack(pieces(gain)), ((0, 5), (0, 0)))
    tilt = jnp.sum(dot(gains, up_full, (1, 0)), axis=0)
    tilt = jnp.stack(pieces(tilt)).reshape(3 * n_gz, -1)
    spare = LANES - tilt.shape[1]
    tilt = jnp.pad(tilt, ((0, block - tilt.shape[0]), (0, 0)))
    marks = columns(part_sum, second)
    extra = jnp.concatenate(
        [
            jnp.pad(marks, ((0, 0), (0, spare - marks.shape[1]))).reshape(n_gz, block, spare),
            jnp.broadcast_to(tilt, (n_gz, *tilt.shape)),
        ],
        axis=2,
    )
    pair = jnp.concatenate(
        [
            dot(y, up_full, (1, 0)).astype(BF).reshape(n_gz, block, hid),
            dot(out_rows, down_full, (1, 1)).astype(BF).reshape(n_gz, block, hid),
            extra,
        ],
        axis=2,
    )
    pair = exchange(pair, GZ)
    marks = pair[:, :, 2 * hid : 2 * hid + spare]
    tilts = pair[:, : 3 * n_gz, 2 * hid + spare :].astype(F32)
    tilts = jnp.sum(tilts.reshape(n_gz, 3, n_gz, -1), axis=1).reshape(n_gz, hid)
    means = column(marks, 0) / local
    mean = jnp.sum(means, axis=0) / n_gz
    shift = means - mean
    var = (jnp.sum(column(marks, 1), axis=0) + local * jnp.sum(shift * shift, axis=0)) / width
    inv = lax.rsqrt(var + 1e-05)
    hidden = summed(pair[:, :, :hid]) + sum(
        (shift[i][:, None] * tilts[i][None] for i in range(n_gz))
    )
    hidden = hidden * inv[:, None]
    d_act = summed(pair[:, :, hid : 2 * hid])
    act_f, slope = gelu_pair(hidden)
    d_hidden = (d_act * slope).astype(BF)
    cross = jnp.sum(d_hidden.astype(F32) * hidden, axis=1)
    marks = columns(cross, mean, inv)
    marks = jnp.pad(marks, ((0, 0), (0, LANES - marks.shape[1])))
    acts = jnp.concatenate([act_f.astype(BF), d_hidden, marks], axis=1)
    acts = spread(acts, GZ).reshape(all_rows, -1)
    act_rows, hgrad_rows, marks = (acts[:, :hid], acts[:, hid : 2 * hid], acts[:, 2 * hid :])
    cross, mean, inv = (column(marks, i) for i in range(3))
    normed = (x_rows - mean[:, None]) * inv[:, None]
    z = (normed * gain).astype(BF)
    dz_part = dot(hgrad_rows, up_full, (1, 1))
    level = jnp.sum(hgrad_rows.astype(F32) * jnp.sum(tilts, axis=0), axis=1)
    marks = columns(level, cross)
    tail = jnp.concatenate(
        [dz_part.astype(BF), jnp.pad(marks, ((0, 0), (0, LANES - marks.shape[1])))], axis=1
    ).reshape(n_gx, rows, local + LANES)
    gain_part = jnp.stack(pieces(jnp.sum(dz_part * normed, axis=0)))
    gain_part = jnp.pad(gain_part, ((0, 5), (0, LANES)))
    tail = jnp.concatenate([tail, jnp.broadcast_to(gain_part, (n_gx, *gain_part.shape))], axis=1)
    tail, acts = lax.optimization_barrier((tail, acts))
    act_rows, hgrad_rows = (acts[:, :hid], acts[:, hid : 2 * hid])
    tail = exchange(tail, "gx")

    def chunks(value, height):
        cut = [value[:, i : i + LANES] for i in range(0, value.shape[1], LANES)]
        return [c.reshape(n_yl, 2, height, LANES) for c in cut]

    grads = jnp.concatenate(
        [
            *chunks(dot(act_rows, out_rows, (0, 0)).astype(BF), down_rows),
            *chunks(dot(z, hgrad_rows, (0, 0)).astype(BF), up_rows),
        ],
        axis=2,
    )
    keep = jnp.where(even, grads[:, 0], grads[:, 1])
    give = jnp.where(even, grads[:, 1], grads[:, 0])
    grads = (keep.astype(F32) + other_core(give).astype(F32)).astype(BF)
    place = lax.axis_index("yl")

    def part(index):
        return lax.dynamic_index_in_dim(grads, index, keepdims=False)

    grads = [part(place)] + [swap(part(place ^ k), "yl", k) for k in range(1, n_yl)]
    d_z = summed(tail[:, :rows, :local])
    marks = summed(tail[:, :rows, local:])
    scaled_sum, cross_sum = (column(marks, i)[:, None] / width for i in range(2))
    d_gain = jnp.sum(tail[:, rows : rows + 3, :local].astype(F32), axis=(0, 1))
    for axis, bits in (("yl", 1), ("yl", 2), ("co", 1)):
        d_gain = d_gain + swap(d_gain, axis, bits)

    def unchunk(first, height, count):
        cut = [slice(first + i * height, first + (i + 1) * height) for i in range(count)]
        cut = [sum((g[c].astype(F32) for g in grads)) for c in cut]
        return jnp.concatenate([c.astype(BF) for c in cut], axis=1)

    d_w_down = unchunk(0, down_rows, local // LANES)
    d_w_up = unchunk(down_rows * (local // LANES), up_rows, hid // LANES)
    first = lax.axis_index("gx") * rows

    def own(values):
        return lax.dynamic_slice(values, (first,), (rows,))[:, None]

    own_inv = own(inv)
    own_normed = (x_in.astype(F32) - own(mean)) * own_inv
    d_x = own_inv * (d_z * gain - scaled_sum - own_normed * cross_sum)
    return (d_x.astype(BF), d_w_up, d_w_down, d_gain)


def solution(mesh):
    sizes = mesh.shape
    cores, x_chips = (2, sizes["gz"] // 2)
    fine = Mesh(
        mesh.devices.reshape(sizes["gx"], sizes["gy"] // cores, cores, 2, x_chips), ("gx", *GY, *GZ)
    )
    placed = (
        P((*GY, "gx"), GZ),
        P(GZ),
        P((*GZ, *GY), "gx"),
        P(("gx", *GY), GZ),
        P((*GY, "gx"), GZ),
    )
    return jax.shard_map(
        body,
        mesh=fine,
        in_specs=placed,
        out_specs=(P((*GY, "gx"), GZ), P((*GZ, *GY), "gx"), P(("gx", *GY), GZ), P(GZ)),
        check_vma=False,
    )
```

profile of v0, /device:TPU:1, one launch (start us, length us, event | category | flops | bytes accessed | tf_op | source)
XLA Modules:
  0.0 213.0 jit_solution(7166205176979230896)
XLA Ops:
  7.9 1.8 broadcast_in_dim.8
  9.7 5.4 %all-to-all-start = ((bf16[4,80,896]{2,1,0:T(8,128)(2,1)}), bf16[4,80,896]{2,1,0:T(8,128)(2,1)S(1)}, u32[]{:S(2)}, u32[]{:S(2)}) async-start(bf16[4,80,896]{2,1,0:T(8,128)(2,1)} %broadcast_in_dim.8), calls=%async_computation | async-start | bytes 1146880 | tf_op jit(solution)/shard_map/all_to_all | solution.py:19
  15.2 28.2 %all_gather.6 = bf16[384,1280]{1,0:T(8,128)(2,1)S(1)} all-gather(bf16[48,1280]{1,0:T(8,128)(2,1)S(1)} %pad_maximum_fusion.2), channel_id=1, replica_groups=mesh['gx'=8,'yl'=4,'co'=2,'yh'=2,'xx'=4] {'gx'}, dimensions={0}, use_global_device_ids=true | all-gather | bytes 1105920 | tf_op jit(solution)/shard_map/all_gather | solution.py:76
  43.4 7.5 %collective-permute-start = (bf16[4,80,896]{2,1,0:T(8,128)(2,1)S(1)}, bf16[4,80,896]{2,1,0:T(8,128)(2,1)S(1)}, u32[]{:S(2)}, u32[]{:S(2)}) collective-permute-start(bf16[4,80,896]{2,1,0:T(8,128)(2,1)S(1)} %all-to-all-done), channel_id=1, source_target_pairs={{0,8},{8,0},{1,9},{9,1},{2,10},{10,2},{3,11},{11,3},{4,12},{12,4},... | collective-permute-start | bytes 1720328 | tf_op jit(solution)/shard_map/ppermute | solution.py:47
  51.7 0.9 collective-permute-done
  53.2 1.7 convolution_convert_fusion.3
  55.0 2.9 %convolution_convert_fusion.2 = bf16[384,896]{1,0:T(8,128)(2,1)} fusion(bf16[896,640]{1,0:T(8,128)(2,1)} %all-gather.2.cloned.1.call-done, bf16[384,1280]{1,0:T(8,128)(2,1)S(1)} %all_gather.6), kind=kOutput, calls=%fused_computation.10 | convolution fusion | flops 440745984 | bytes 2326528 | tf_op jit(solution)/shard_map/dot_general | solution.py:55
  57.9 2.1 %concatenate.25 = bf16[8,48,1920]{2,1,0:T(8,128)(2,1)S(1)} concatenate(bf16[8,48,896]{2,1,0:T(8,128)(2,1)S(1)} %bitcast.163, bf16[8,48,896]{2,1,0:T(8,128)(2,1)} %bitcast.164, bf16[8,48,16]{2,1,0:T(8,128)(2,1)S(1)} %bitcast.172, bf16[8,48,112]{2,1,0:T(8,128)(2,1)S(1)} %broadcast_in_dim.9), dimensions={2} | concatenate | bytes 2949120 | tf_op jit(solution)/shard_map/concatenate | solution.py:97
  60.1 31.1 %all_to_all.20 = bf16[8,48,1920]{2,1,0:T(8,128)(2,1)S(1)} all-to-all(bf16[8,48,1920]{2,1,0:T(8,128)(2,1)S(1)} %concatenate.25), channel_id=1, replica_groups=mesh['gx'=8,'yl'=4,'co'=2,'yh'=2,'xx'=4] {'yh','xx'}, dimensions={0} | all-to-all | bytes 2949120 | tf_op jit(solution)/shard_map/all_to_all | solution.py:19
  93.1 1.2 broadcast_in_dim.10
  94.3 4.3 %all-to-all-start.2 = ((bf16[8,48,1920]{2,1,0:T(8,128)(2,1)}), bf16[8,48,1920]{2,1,0:T(8,128)(2,1)}, u32[]{:S(2)}, u32[]{:S(2)}) async-start(bf16[8,48,1920]{2,1,0:T(8,128)(2,1)} %broadcast_in_dim.10), calls=%async_computation.2 | async-start | bytes 2949120 | tf_op jit(solution)/shard_map/all_to_all | solution.py:19
  98.8 15.7 %all-to-all-done.2 = bf16[8,48,1920]{2,1,0:T(8,128)(2,1)} async-done(((bf16[8,48,1920]{2,1,0:T(8,128)(2,1)}), bf16[8,48,1920]{2,1,0:T(8,128)(2,1)}, u32[]{:S(2)}, u32[]{:S(2)}) %all-to-all-start.2) | async-done | bytes 1474592 | tf_op jit(solution)/shard_map/all_to_all | solution.py:19
  114.4 1.2 fusion.108
  115.6 1.3 multiply_reduce_fusion
  117.4 2.1 fusion.111
  119.8 0.9 pad_maximum_fusion.1
  120.7 2.1 convolution_convert_fusion
  122.8 1.9 convolution_convert_fusion.1
  125.7 19.9 %collective-permute-start.1 = (bf16[4,1120,128]{2,1,0:T(8,128)(2,1)S(1)}, bf16[4,1120,128]{2,1,0:T(8,128)(2,1)}, u32[]{:S(2)}, u32[]{:S(2)}) collective-permute-start(bf16[4,1120,128]{2,1,0:T(8,128)(2,1)S(1)} %select_bitcast_fusion), channel_id=1, source_target_pairs={{0,8},{8,0},{1,9},{9,1},{2,10},{10,2},{3,11},{11,3},{4,12},{12,4},... | collective-permute-start | bytes 3440648 | tf_op jit(solution)/shard_map/ppermute | solution.py:47
  145.6 4.2 %all-to-all-start.3 = ((bf16[8,56,768]{2,1,0:T(8,128)(2,1)}), bf16[8,56,768]{2,1,0:T(8,128)(2,1)}, u32[]{:S(2)}, u32[]{:S(2)}) async-start(bf16[8,56,768]{2,1,0:T(8,128)(2,1)} %pad_maximum_fusion.1), calls=%async_computation.3 | async-start | bytes 1376256 | tf_op jit(solution)/shard_map/all_to_all | solution.py:19
  150.0 1.7 fusion
  151.8 20.0 %collective-permute-start.2 = (bf16[1120,128]{1,0:T(8,128)(2,1)S(1)}, bf16[1120,128]{1,0:T(8,128)(2,1)S(1)}, u32[]{:S(2)}, u32[]{:S(2)}) collective-permute-start(bf16[1120,128]{1,0:T(8,128)(2,1)S(1)} %get-tuple-element.29), channel_id=1, source_target_pairs={{0,16},{16,0},{32,48},{48,32},{1,17},{17,1},{33,49},{49,33},{2,18}... | collective-permute-start | bytes 860168 | tf_op jit(solution)/shard_map/ppermute | solution.py:47
  171.8 2.0 collective-permute-start.4
  173.8 3.0 %collective-permute-start.3 = (bf16[1120,128]{1,0:T(8,128)(2,1)S(1)}, bf16[1120,128]{1,0:T(8,128)(2,1)S(1)}, u32[]{:S(2)}, u32[]{:S(2)}) collective-permute-start(bf16[1120,128]{1,0:T(8,128)(2,1)S(1)} %get-tuple-element.31), channel_id=1, source_target_pairs={{0,32},{16,48},{32,0},{48,16},{1,33},{17,49},{33,1},{49,17},{2,34}... | collective-permute-start | bytes 860168 | tf_op jit(solution)/shard_map/ppermute | solution.py:47
  176.8 0.9 convert_reduce_fusion.8
  177.7 14.6 %collective-permute-start.5 = (f32[640]{0:T(1024)S(1)}, f32[640]{0:T(1024)S(1)}, u32[]{:S(2)}, u32[]{:S(2)}) collective-permute-start(f32[640]{0:T(1024)S(1)} %convert_reduce_fusion.8), channel_id=1, source_target_pairs={{0,16},{16,0},{32,48},{48,32},{1,17},{17,1},{33,49},{49,33},{2,18}... | collective-permute-start | bytes 7688 | tf_op jit(solution)/shard_map/ppermute | solution.py:47
  192.3 0.9 convert_reduce_fusion.4
  193.5 2.5 %collective-permute-start.6 = (f32[640]{0:T(1024)S(1)}, f32[640]{0:T(1024)S(1)}, u32[]{:S(2)}, u32[]{:S(2)}) collective-permute-start(f32[640]{0:T(1024)S(1)} %add.288), channel_id=1, source_target_pairs={{0,32},{16,48},{32,0},{48,16},{1,33},{17,49},{33,1},{49,17},{2,34}... | collective-permute-start | bytes 7688 | tf_op jit(solution)/shard_map/ppermute | solution.py:47
  195.9 1.1 convert_reduce_fusion.3
  197.0 3.0 %collective-permute-done.6 = f32[640]{0:T(1024)S(1)} collective-permute-done((f32[640]{0:T(1024)S(1)}, f32[640]{0:T(1024)S(1)}, u32[]{:S(2)}, u32[]{:S(2)}) %collective-permute-start.6) | collective-permute-done | bytes 2592 | tf_op jit(solution)/shard_map/ppermute | solution.py:47
  200.1 3.0 %collective-permute-start.7 = (f32[640]{0:T(1024)S(1)}, f32[640]{0:T(1024)S(1)}, u32[]{:S(2)}, u32[]{:S(2)}) collective-permute-start(f32[640]{0:T(1024)S(1)} %add.289), channel_id=1, source_target_pairs={{0,8},{8,0},{1,9},{9,1},{2,10},{10,2},{3,11},{11,3},{4,12},{12,4},... | collective-permute-start | bytes 7688 | tf_op jit(solution)/shard_map/ppermute | solution.py:47
  203.1 0.7 multiply_convert_fusion.1
  (129 shorter events, 8.3 us)
Async XLA Ops:
  7.2 8.0 %copy-start.7 = (f32[640]{0:T(1024)S(1)}, f32[640]{0:T(1024)}, u32[]{:S(2)}) copy-start(f32[640]{0:T(1024)} %param.6) | copy-start | bytes 7684
  7.2 8.0 %copy-start.5 = (bf16[48,640]{1,0:T(8,128)(2,1)S(1)}, bf16[48,640]{1,0:T(8,128)(2,1)}, u32[]{:S(2)}) copy-start(bf16[48,640]{1,0:T(8,128)(2,1)} %param.5) | copy-start | bytes 184324
  7.2 8.0 %copy-start.6 = (bf16[48,640]{1,0:T(8,128)(2,1)S(1)}, bf16[48,640]{1,0:T(8,128)(2,1)}, u32[]{:S(2)}) copy-start(bf16[48,640]{1,0:T(8,128)(2,1)} %param.9) | copy-start | bytes 184324
  7.2 47.8 %all-gather.2.cloned.1.call-start = ((), (), s32[]{:S(2)}) async-start(), calls=%async_computation.4 | async-start | bytes 1290240 | tf_op jit(solution)/shard_map/all_gather | solution.py:74
  9.7 33.7 %all-to-all-start = ((bf16[4,80,896]{2,1,0:T(8,128)(2,1)}), bf16[4,80,896]{2,1,0:T(8,128)(2,1)S(1)}, u32[]{:S(2)}, u32[]{:S(2)}) async-start(bf16[4,80,896]{2,1,0:T(8,128)(2,1)} %broadcast_in_dim.8), calls=%async_computation | async-start | bytes 1146880 | tf_op jit(solution)/shard_map/all_to_all | solution.py:19
  43.4 11.5 %copy-start.2 = (bf16[384,1280]{1,0:T(8,128)(2,1)}, bf16[384,1280]{1,0:T(8,128)(2,1)S(1)}, u32[]{:S(2)}) copy-start(bf16[384,1280]{1,0:T(8,128)(2,1)S(1)} %all_gather.6) | copy-start | bytes 2949124
  43.4 9.1 %collective-permute-start = (bf16[4,80,896]{2,1,0:T(8,128)(2,1)S(1)}, bf16[4,80,896]{2,1,0:T(8,128)(2,1)S(1)}, u32[]{:S(2)}, u32[]{:S(2)}) collective-permute-start(bf16[4,80,896]{2,1,0:T(8,128)(2,1)S(1)} %all-to-all-done), channel_id=1, source_target_pairs={{0,8},{8,0},{1,9},{9,1},{2,10},{10,2},{3,11},{11,3},{4,12},{12,4},... | collective-permute-start | bytes 1720328 | tf_op jit(solution)/shard_map/ppermute | solution.py:47
  52.8 2.2 %copy-start = (bf16[4,2,80,896]{3,2,1,0:T(8,128)(2,1)}, bf16[4,2,80,896]{3,2,1,0:T(8,128)(2,1)S(1)}, u32[]{:S(2)}) copy-start(bf16[4,2,80,896]{3,2,1,0:T(8,128)(2,1)S(1)} %pad_maximum_fusion) | copy-start | bytes 3440644
  55.0 3.0 %copy-start.4 = (bf16[384,896]{1,0:T(8,128)(2,1)S(1)}, bf16[384,896]{1,0:T(8,128)(2,1)}, u32[]{:S(2)}) copy-start(bf16[384,896]{1,0:T(8,128)(2,1)} %convolution_convert_fusion.3) | copy-start | bytes 2064388
  94.3 20.2 %all-to-all-start.2 = ((bf16[8,48,1920]{2,1,0:T(8,128)(2,1)}), bf16[8,48,1920]{2,1,0:T(8,128)(2,1)}, u32[]{:S(2)}, u32[]{:S(2)}) async-start(bf16[8,48,1920]{2,1,0:T(8,128)(2,1)} %broadcast_in_dim.10), calls=%async_computation.2 | async-start | bytes 2949120 | tf_op jit(solution)/shard_map/all_to_all | solution.py:19
  98.6 18.8 %copy-start.1 = (bf16[4,2,80,896]{3,2,1,0:T(8,128)(2,1)S(1)}, bf16[4,2,80,896]{3,2,1,0:T(8,128)(2,1)}, u32[]{:S(2)}) copy-start(bf16[4,2,80,896]{3,2,1,0:T(8,128)(2,1)} %copy-done) | copy-start | bytes 3440644
  119.5 1.2 copy-start.3
  125.7 24.3 %collective-permute-start.1 = (bf16[4,1120,128]{2,1,0:T(8,128)(2,1)S(1)}, bf16[4,1120,128]{2,1,0:T(8,128)(2,1)}, u32[]{:S(2)}, u32[]{:S(2)}) collective-permute-start(bf16[4,1120,128]{2,1,0:T(8,128)(2,1)S(1)} %select_bitcast_fusion), channel_id=1, source_target_pairs={{0,8},{8,0},{1,9},{9,1},{2,10},{10,2},{3,11},{11,3},{4,12},{12,4},... | collective-permute-start | bytes 3440648 | tf_op jit(solution)/shard_map/ppermute | solution.py:47
  145.6 31.2 %all-to-all-start.3 = ((bf16[8,56,768]{2,1,0:T(8,128)(2,1)}), bf16[8,56,768]{2,1,0:T(8,128)(2,1)}, u32[]{:S(2)}, u32[]{:S(2)}) async-start(bf16[8,56,768]{2,1,0:T(8,128)(2,1)} %pad_maximum_fusion.1), calls=%async_computation.3 | async-start | bytes 1376256 | tf_op jit(solution)/shard_map/all_to_all | solution.py:19
  151.8 52.7 %collective-permute-start.2 = (bf16[1120,128]{1,0:T(8,128)(2,1)S(1)}, bf16[1120,128]{1,0:T(8,128)(2,1)S(1)}, u32[]{:S(2)}, u32[]{:S(2)}) collective-permute-start(bf16[1120,128]{1,0:T(8,128)(2,1)S(1)} %get-tuple-element.29), channel_id=1, source_target_pairs={{0,16},{16,0},{32,48},{48,32},{1,17},{17,1},{33,49},{49,33},{2,18}... | collective-permute-start | bytes 860168 | tf_op jit(solution)/shard_map/ppermute | solution.py:47
  171.8 32.7 %collective-permute-start.4 = (bf16[1120,128]{1,0:T(8,128)(2,1)S(1)}, bf16[1120,128]{1,0:T(8,128)(2,1)S(1)}, u32[]{:S(2)}, u32[]{:S(2)}) collective-permute-start(bf16[1120,128]{1,0:T(8,128)(2,1)S(1)} %get-tuple-element.30), channel_id=1, source_target_pairs={{0,48},{16,32},{32,16},{48,0},{1,49},{17,33},{33,17},{49,1},{2,50}... | collective-permute-start | bytes 860168 | tf_op jit(solution)/shard_map/ppermute | solution.py:47
  173.8 30.7 %collective-permute-start.3 = (bf16[1120,128]{1,0:T(8,128)(2,1)S(1)}, bf16[1120,128]{1,0:T(8,128)(2,1)S(1)}, u32[]{:S(2)}, u32[]{:S(2)}) collective-permute-start(bf16[1120,128]{1,0:T(8,128)(2,1)S(1)} %get-tuple-element.31), channel_id=1, source_target_pairs={{0,32},{16,48},{32,0},{48,16},{1,33},{17,49},{33,1},{49,17},{2,34}... | collective-permute-start | bytes 860168 | tf_op jit(solution)/shard_map/ppermute | solution.py:47
  177.7 15.7 %collective-permute-start.5 = (f32[640]{0:T(1024)S(1)}, f32[640]{0:T(1024)S(1)}, u32[]{:S(2)}, u32[]{:S(2)}) collective-permute-start(f32[640]{0:T(1024)S(1)} %convert_reduce_fusion.8), channel_id=1, source_target_pairs={{0,16},{16,0},{32,48},{48,32},{1,17},{17,1},{33,49},{49,33},{2,18}... | collective-permute-start | bytes 7688 | tf_op jit(solution)/shard_map/ppermute | solution.py:47
  193.5 6.6 %collective-permute-start.6 = (f32[640]{0:T(1024)S(1)}, f32[640]{0:T(1024)S(1)}, u32[]{:S(2)}, u32[]{:S(2)}) collective-permute-start(f32[640]{0:T(1024)S(1)} %add.288), channel_id=1, source_target_pairs={{0,32},{16,48},{32,0},{48,16},{1,33},{17,49},{33,1},{49,17},{2,34}... | collective-permute-start | bytes 7688 | tf_op jit(solution)/shard_map/ppermute | solution.py:47
  200.1 3.8 %collective-permute-start.7 = (f32[640]{0:T(1024)S(1)}, f32[640]{0:T(1024)S(1)}, u32[]{:S(2)}, u32[]{:S(2)}) collective-permute-start(f32[640]{0:T(1024)S(1)} %add.289), channel_id=1, source_target_pairs={{0,8},{8,0},{1,9},{9,1},{2,10},{10,2},{3,11},{11,3},{4,12},{12,4},... | collective-permute-start | bytes 7688 | tf_op jit(solution)/shard_map/ppermute | solution.py:47
  204.8 0.7 copy-start.9
  205.5 0.7 copy-start.8
Sparse Core Ops, SparseCore 0:
  10.1 43.4 all-gather.1
where the time goes:
time: 214 us; the launch traced here: 213 us
  starting transfers between devices  86.4 us (40%)
  blocking collectives  59.3 us (28%)
  waiting for transfers between devices  20.4 us (10%)
  between operations  14.7 us (7%)
  matrix products  11 us (5%)
  other arithmetic  10.9 us (5%)
  local copies, waits for them, and re-layouts  10.2 us (5%)
    ppermute x8, starting transfers between devices, swap(): lax.ppermute(value, axis, [(i, i ^ bits) for i in range(lax.axis_size(axi...  72.5 us
    all_to_all x1, blocking collectives, exchange(): return lax.all_to_all(blocks, axis, 0, 0, tiled=True)  31.1 us
    all_gather x1, blocking collectives, body(): lax.all_gather(jnp.concatenate([x_in, d_out], axis=1), 'gx', axis=0, tile...  28.2 us
    all_to_all x3, waiting for transfers between devices, exchange(): return lax.all_to_all(blocks, axis, 0, 0, tiled=True)  15.7 us
    all_to_all x3, starting transfers between devices, exchange(): return lax.all_to_all(blocks, axis, 0, 0, tiled=True)  13.9 us
    dot_general x6, matrix products, dot(): lax.dot_general(a, b, ((contract[:1], contract[1:]), ((), ())), preferred...  11 us
  transfers between devices with their start and end apart: 12, of which 4 were waited for; matrix products, arithmetic and copies ran while one was open for 5% of the time, Pallas kernels for 0%

commit v1 on v0

--- a/solution.py
+++ b/solution.py
@@ -73,7 +73,12 @@
 
     down_full = lax.all_gather(w_down, GY, axis=0, tiled=True)
     up_mine = spread(w_up, "yl")
-    both = lax.all_gather(jnp.concatenate([x_in, d_out], axis=1), "gx", axis=0, tiled=True)
+    both = jnp.concatenate(
+        lax.all_to_all(
+            jnp.stack([jnp.concatenate([x_in, d_out], axis=1)] * lax.axis_size("gx")), "gx", 0, 0
+        ),
+        axis=0,
+    )
     both, up_mine = lax.optimization_barrier((both, up_mine))
     up_full = by_core(up_mine, other_core(up_mine))
     x_rows, out_rows = (both[:, :local].astype(F32), both[:, local:])

time: 214 us -> 240 us (1.12)
  waiting for transfers between devices: 20.4 us -> 91.1 us
  starting transfers between devices: 86.4 us -> 56 us
  blocking collectives: 59.3 us -> 43 us
    ppermute x8, starting transfers between devices: 72.5 us -> 24.2 us  [swap(): lax.ppermute(value, axis, [(i, i ^ bits) for i in range(lax.axis_size(axi...]
    all_to_all x3, waiting for transfers between devices: 15.7 us -> 48.1 us  [exchange(): return lax.all_to_all(blocks, axis, 0, 0, tiled=True)]
    all_gather x1 -> x0, blocking collectives: 28.2 us -> none  [body(): lax.all_gather(jnp.concatenate([x_in, d_out], axis=1), 'gx', axis=0, tile...]
    all_to_all x0 -> x1, waiting for transfers between devices: none -> 27 us  [body(): lax.all_to_all(jnp.stack([jnp.concatenate([x_in, d_out], axis=1)] * lax.a...]
    all_to_all x0 -> x1, starting transfers between devices: none -> 13.4 us  [body(): lax.all_to_all(jnp.stack([jnp.concatenate([x_in, d_out], axis=1)] * lax.a...]
    all_to_all x1, blocking collectives: 31.1 us -> 43 us  [exchange(): return lax.all_to_all(blocks, axis, 0, 0, tiled=True)]
    all_gather x1, waiting for transfers between devices: 0.01 us -> 11.4 us  [body(): down_full = lax.all_gather(w_down, GY, axis=0, tiled=True)]
    all_to_all x3, starting transfers between devices: 13.9 us -> 18.4 us  [exchange(): return lax.all_to_all(blocks, axis, 0, 0, tiled=True)]
  transfers between devices with their start and end apart: 12 -> 13, of which waited for: 4 -> 8; matrix products, arithmetic and copies ran while one was open for 5% -> 4% of each run, Pallas kernels for 0% -> 0%
where the time goes in v1:
time: 240 us; the launch traced here: 239 us
  waiting for transfers between devices  91.1 us (38%)
  starting transfers between devices  56 us (23%)
  blocking collectives  43 us (18%)
  between operations  14.6 us (6%)
  local copies, waits for them, and re-layouts  11.9 us (5%)
  other arithmetic  11.1 us (5%)
  matrix products  11 us (5%)
    all_to_all x3, waiting for transfers between devices, exchange(): return lax.all_to_all(blocks, axis, 0, 0, tiled=True)  48.1 us
    all_to_all x1, blocking collectives, exchange(): return lax.all_to_all(blocks, axis, 0, 0, tiled=True)  43 us
    all_to_all x1, waiting for transfers between devices, body(): lax.all_to_all(jnp.stack([jnp.concatenate([x_in, d_out], axis=1)] * lax.a...  27 us
    ppermute x8, starting transfers between devices, swap(): lax.ppermute(value, axis, [(i, i ^ bits) for i in range(lax.axis_size(axi...  24.2 us
    all_to_all x3, starting transfers between devices, exchange(): return lax.all_to_all(blocks, axis, 0, 0, tiled=True)  18.4 us
    all_to_all x1, starting transfers between devices, body(): lax.all_to_all(jnp.stack([jnp.concatenate([x_in, d_out], axis=1)] * lax.a...  13.4 us
    all_gather x1, waiting for transfers between devices, body(): down_full = lax.all_gather(w_down, GY, axis=0, tiled=True)  11.4 us
    dot_general x6, matrix products, dot(): lax.dot_general(a, b, ((contract[:1], contract[1:]), ((), ())), preferred...  11 us
  transfers between devices with their start and end apart: 13, of which 8 were waited for; matrix products, arithmetic and copies ran while one was open for 4% of the time, Pallas kernels for 0%

profile of v1, /device:TPU:1, one launch (start us, length us, event | category | flops | bytes accessed | tf_op | source)
XLA Modules:
  0.0 238.7 jit_solution(14245137097369560397)
XLA Ops:
  7.2 1.8 broadcast_in_dim.8
  9.0 5.4 %all-to-all-start.1 = ((bf16[4,80,896]{2,1,0:T(8,128)(2,1)}), bf16[4,80,896]{2,1,0:T(8,128)(2,1)S(1)}, u32[]{:S(2)}, u32[]{:S(2)}) async-start(bf16[4,80,896]{2,1,0:T(8,128)(2,1)} %broadcast_in_dim.8), calls=%async_computation.1 | async-start | bytes 1146880 | tf_op jit(solution)/shard_map/all_to_all | solution.py:19
  14.4 11.6 %all-to-all-done.1 = bf16[4,80,896]{2,1,0:T(8,128)(2,1)S(1)} async-done(((bf16[4,80,896]{2,1,0:T(8,128)(2,1)}), bf16[4,80,896]{2,1,0:T(8,128)(2,1)S(1)}, u32[]{:S(2)}, u32[]{:S(2)}) %all-to-all-start.1) | async-done | bytes 573472 | tf_op jit(solution)/shard_map/all_to_all | solution.py:19
  27.1 13.4 %all-to-all-start = ((bf16[8,48,1280]{2,1,0:T(8,128)(2,1)}), bf16[8,48,1280]{2,1,0:T(8,128)(2,1)S(1)}, u32[]{:S(2)}, u32[]{:S(2)}) async-start(bf16[8,48,1280]{2,1,0:T(8,128)(2,1)} %stack.26), calls=%async_computation | async-start | bytes 1966080 | tf_op jit(solution)/shard_map/all_to_all | solution.py:77
  41.4 27.0 %all-to-all-done = bf16[8,48,1280]{2,1,0:T(8,128)(2,1)S(1)} async-done(((bf16[8,48,1280]{2,1,0:T(8,128)(2,1)}), bf16[8,48,1280]{2,1,0:T(8,128)(2,1)S(1)}, u32[]{:S(2)}, u32[]{:S(2)}) %all-to-all-start) | async-done | bytes 983072 | tf_op jit(solution)/shard_map/all_to_all | solution.py:77
  68.3 2.4 %collective-permute-start = (bf16[4,80,896]{2,1,0:T(8,128)(2,1)S(1)}, bf16[4,80,896]{2,1,0:T(8,128)(2,1)S(1)}, u32[]{:S(2)}, u32[]{:S(2)}) collective-permute-start(bf16[4,80,896]{2,1,0:T(8,128)(2,1)S(1)} %all-to-all-done.1), channel_id=1, source_target_pairs={{0,8},{8,0},{1,9},{9,1},{2,10},{10,2},{3,11},{11,3},{4,12},{12,4},... | collective-permute-start | bytes 1720328 | tf_op jit(solution)/shard_map/ppermute | solution.py:47
  71.5 11.4 %all-gather.2.cloned.1.call-done = bf16[896,640]{1,0:T(8,128)(2,1)} async-done(((bf16[112,640]{1,0:T(8,128)(2,1)}), bf16[896,640]{1,0:T(8,128)(2,1)}) %all-gather.2.cloned.1.call-update) | async-done | bytes 1146896 | tf_op jit(solution)/shard_map/all_gather | solution.py:74
  82.8 2.9 %convolution_convert_fusion.2 = bf16[384,896]{1,0:T(8,128)(2,1)} fusion(bf16[896,640]{1,0:T(8,128)(2,1)} %all-gather.2.cloned.1.call-done, bf16[384,1280]{1,0:T(8,128)(2,1)S(1)} %bitcast.160), kind=kOutput, calls=%fused_computation.10 | convolution fusion | flops 440745984 | bytes 2326528 | tf_op jit(solution)/shard_map/dot_general | solution.py:55
  86.0 1.7 convolution_convert_fusion.3
  88.8 2.1 concatenate.25
  90.9 43.0 %all_to_all.25 = bf16[8,48,1920]{2,1,0:T(8,128)(2,1)S(1)} all-to-all(bf16[8,48,1920]{2,1,0:T(8,128)(2,1)S(1)} %concatenate.25), channel_id=1, replica_groups=mesh['gx'=8,'yl'=4,'co'=2,'yh'=2,'xx'=4] {'yh','xx'}, dimensions={0} | all-to-all | bytes 2949120 | tf_op jit(solution)/shard_map/all_to_all | solution.py:19
  135.8 1.2 broadcast_in_dim.10
  137.0 6.2 %all-to-all-start.3 = ((bf16[8,48,1920]{2,1,0:T(8,128)(2,1)}), bf16[8,48,1920]{2,1,0:T(8,128)(2,1)}, u32[]{:S(2)}, u32[]{:S(2)}) async-start(bf16[8,48,1920]{2,1,0:T(8,128)(2,1)} %broadcast_in_dim.10), calls=%async_computation.3 | async-start | bytes 2949120 | tf_op jit(solution)/shard_map/all_to_all | solution.py:19
  143.4 25.3 %all-to-all-done.3 = bf16[8,48,1920]{2,1,0:T(8,128)(2,1)} async-done(((bf16[8,48,1920]{2,1,0:T(8,128)(2,1)}), bf16[8,48,1920]{2,1,0:T(8,128)(2,1)}, u32[]{:S(2)}, u32[]{:S(2)}) %all-to-all-start.3) | async-done | bytes 1474592 | tf_op jit(solution)/shard_map/all_to_all | solution.py:19
  168.7 1.2 fusion.108
  169.9 1.3 multiply_reduce_fusion
  171.6 2.1 fusion.111
  175.0 2.1 convolution_convert_fusion
  177.0 2.0 convolution_convert_fusion.1
  179.9 5.3 %collective-permute-start.1 = (bf16[4,1120,128]{2,1,0:T(8,128)(2,1)S(1)}, bf16[4,1120,128]{2,1,0:T(8,128)(2,1)}, u32[]{:S(2)}, u32[]{:S(2)}) collective-permute-start(bf16[4,1120,128]{2,1,0:T(8,128)(2,1)S(1)} %select_bitcast_fusion), channel_id=1, source_target_pairs={{0,8},{8,0},{1,9},{9,1},{2,10},{10,2},{3,11},{11,3},{4,12},{12,4},... | collective-permute-start | bytes 3440648 | tf_op jit(solution)/shard_map/ppermute | solution.py:47
  185.3 6.8 %all-to-all-start.4 = ((bf16[8,56,768]{2,1,0:T(8,128)(2,1)}), bf16[8,56,768]{2,1,0:T(8,128)(2,1)}, u32[]{:S(2)}, u32[]{:S(2)}) async-start(bf16[8,56,768]{2,1,0:T(8,128)(2,1)} %pad_maximum_fusion.1), calls=%async_computation.4 | async-start | bytes 1376256 | tf_op jit(solution)/shard_map/all_to_all | solution.py:19
  192.2 1.8 fusion
  194.1 1.9 collective-permute-start.2
  196.0 3.7 %collective-permute-start.4 = (bf16[1120,128]{1,0:T(8,128)(2,1)S(1)}, bf16[1120,128]{1,0:T(8,128)(2,1)S(1)}, u32[]{:S(2)}, u32[]{:S(2)}) collective-permute-start(bf16[1120,128]{1,0:T(8,128)(2,1)S(1)} %get-tuple-element.30), channel_id=1, source_target_pairs={{0,48},{16,32},{32,16},{48,0},{1,49},{17,33},{33,17},{49,1},{2,50}... | collective-permute-start | bytes 860168 | tf_op jit(solution)/shard_map/ppermute | solution.py:47
  199.7 2.8 %collective-permute-start.3 = (bf16[1120,128]{1,0:T(8,128)(2,1)S(1)}, bf16[1120,128]{1,0:T(8,128)(2,1)S(1)}, u32[]{:S(2)}, u32[]{:S(2)}) collective-permute-start(bf16[1120,128]{1,0:T(8,128)(2,1)S(1)} %get-tuple-element.31), channel_id=1, source_target_pairs={{0,32},{16,48},{32,0},{48,16},{1,33},{17,49},{33,1},{49,17},{2,34}... | collective-permute-start | bytes 860168 | tf_op jit(solution)/shard_map/ppermute | solution.py:47
  202.5 11.2 %all-to-all-done.4 = bf16[8,56,768]{2,1,0:T(8,128)(2,1)} async-done(((bf16[8,56,768]{2,1,0:T(8,128)(2,1)}), bf16[8,56,768]{2,1,0:T(8,128)(2,1)}, u32[]{:S(2)}, u32[]{:S(2)}) %all-to-all-start.4) | async-done | bytes 688160 | tf_op jit(solution)/shard_map/all_to_all | solution.py:19
  214.6 1.9 collective-permute-start.5
  217.6 1.3 collective-permute-done.5
  218.9 2.8 %collective-permute-start.6 = (f32[640]{0:T(1024)S(1)}, f32[640]{0:T(1024)S(1)}, u32[]{:S(2)}, u32[]{:S(2)}) collective-permute-start(f32[640]{0:T(1024)S(1)} %add.288), channel_id=1, source_target_pairs={{0,32},{16,48},{32,0},{48,16},{1,33},{17,49},{33,1},{49,17},{2,34}... | collective-permute-start | bytes 7688 | tf_op jit(solution)/shard_map/ppermute | solution.py:47
  221.7 1.1 convert_reduce_fusion.3
  222.8 2.6 %collective-permute-done.6 = f32[640]{0:T(1024)S(1)} collective-permute-done((f32[640]{0:T(1024)S(1)}, f32[640]{0:T(1024)S(1)}, u32[]{:S(2)}, u32[]{:S(2)}) %collective-permute-start.6) | collective-permute-done | bytes 2592 | tf_op jit(solution)/shard_map/ppermute | solution.py:47
  225.5 3.4 %collective-permute-start.7 = (f32[640]{0:T(1024)S(1)}, f32[640]{0:T(1024)S(1)}, u32[]{:S(2)}, u32[]{:S(2)}) collective-permute-start(f32[640]{0:T(1024)S(1)} %add.289), channel_id=1, source_target_pairs={{0,8},{8,0},{1,9},{9,1},{2,10},{10,2},{3,11},{11,3},{4,12},{12,4},... | collective-permute-start | bytes 7688 | tf_op jit(solution)/shard_map/ppermute | solution.py:47
  (131 shorter events, 13.4 us)
Async XLA Ops:
  7.2 7.2 %copy-start.5 = (bf16[48,640]{1,0:T(8,128)(2,1)S(1)}, bf16[48,640]{1,0:T(8,128)(2,1)}, u32[]{:S(2)}) copy-start(bf16[48,640]{1,0:T(8,128)(2,1)} %param.5) | copy-start | bytes 184324
  7.2 7.2 %copy-start.6 = (bf16[48,640]{1,0:T(8,128)(2,1)S(1)}, bf16[48,640]{1,0:T(8,128)(2,1)}, u32[]{:S(2)}) copy-start(bf16[48,640]{1,0:T(8,128)(2,1)} %param.9) | copy-start | bytes 184324
  9.0 17.1 %all-to-all-start.1 = ((bf16[4,80,896]{2,1,0:T(8,128)(2,1)}), bf16[4,80,896]{2,1,0:T(8,128)(2,1)S(1)}, u32[]{:S(2)}, u32[]{:S(2)}) async-start(bf16[4,80,896]{2,1,0:T(8,128)(2,1)} %broadcast_in_dim.8), calls=%async_computation.1 | async-start | bytes 1146880 | tf_op jit(solution)/shard_map/all_to_all | solution.py:19
  14.4 26.9 %copy-start.7 = (f32[640]{0:T(1024)S(1)}, f32[640]{0:T(1024)}, u32[]{:S(2)}) copy-start(f32[640]{0:T(1024)} %param.6) | copy-start | bytes 7684
  27.1 41.2 %all-to-all-start = ((bf16[8,48,1280]{2,1,0:T(8,128)(2,1)}), bf16[8,48,1280]{2,1,0:T(8,128)(2,1)S(1)}, u32[]{:S(2)}, u32[]{:S(2)}) async-start(bf16[8,48,1280]{2,1,0:T(8,128)(2,1)} %stack.26), calls=%async_computation | async-start | bytes 1966080 | tf_op jit(solution)/shard_map/all_to_all | solution.py:77
  40.5 42.3 %all-gather.2.cloned.1.call-start = ((), (), s32[]{:S(2)}) async-start(), calls=%async_computation.5 | async-start | bytes 1290240 | tf_op jit(solution)/shard_map/all_gather | solution.py:74
  68.3 17.7 %copy-start.2 = (bf16[8,48,1280]{2,1,0:T(8,128)(2,1)}, bf16[8,48,1280]{2,1,0:T(8,128)(2,1)S(1)}, u32[]{:S(2)}) copy-start(bf16[8,48,1280]{2,1,0:T(8,128)(2,1)S(1)} %all-to-all-done) | copy-start | bytes 2949124
  68.3 17.4 %collective-permute-start = (bf16[4,80,896]{2,1,0:T(8,128)(2,1)S(1)}, bf16[4,80,896]{2,1,0:T(8,128)(2,1)S(1)}, u32[]{:S(2)}, u32[]{:S(2)}) collective-permute-start(bf16[4,80,896]{2,1,0:T(8,128)(2,1)S(1)} %all-to-all-done.1), channel_id=1, source_target_pairs={{0,8},{8,0},{1,9},{9,1},{2,10},{10,2},{3,11},{11,3},{4,12},{12,4},... | collective-permute-start | bytes 1720328 | tf_op jit(solution)/shard_map/ppermute | solution.py:47
  86.0 1.7 copy-start
  87.7 1.1 copy-start.4
  137.0 31.6 %all-to-all-start.3 = ((bf16[8,48,1920]{2,1,0:T(8,128)(2,1)}), bf16[8,48,1920]{2,1,0:T(8,128)(2,1)}, u32[]{:S(2)}, u32[]{:S(2)}) async-start(bf16[8,48,1920]{2,1,0:T(8,128)(2,1)} %broadcast_in_dim.10), calls=%async_computation.3 | async-start | bytes 2949120 | tf_op jit(solution)/shard_map/all_to_all | solution.py:19
  143.2 28.4 %copy-start.1 = (bf16[4,2,80,896]{3,2,1,0:T(8,128)(2,1)S(1)}, bf16[4,2,80,896]{3,2,1,0:T(8,128)(2,1)}, u32[]{:S(2)}) copy-start(bf16[4,2,80,896]{3,2,1,0:T(8,128)(2,1)} %copy-done) | copy-start | bytes 3440644
  173.8 1.2 copy-start.3
  179.9 12.3 %collective-permute-start.1 = (bf16[4,1120,128]{2,1,0:T(8,128)(2,1)S(1)}, bf16[4,1120,128]{2,1,0:T(8,128)(2,1)}, u32[]{:S(2)}, u32[]{:S(2)}) collective-permute-start(bf16[4,1120,128]{2,1,0:T(8,128)(2,1)S(1)} %select_bitcast_fusion), channel_id=1, source_target_pairs={{0,8},{8,0},{1,9},{9,1},{2,10},{10,2},{3,11},{11,3},{4,12},{12,4},... | collective-permute-start | bytes 3440648 | tf_op jit(solution)/shard_map/ppermute | solution.py:47
  185.3 28.4 %all-to-all-start.4 = ((bf16[8,56,768]{2,1,0:T(8,128)(2,1)}), bf16[8,56,768]{2,1,0:T(8,128)(2,1)}, u32[]{:S(2)}, u32[]{:S(2)}) async-start(bf16[8,56,768]{2,1,0:T(8,128)(2,1)} %pad_maximum_fusion.1), calls=%async_computation.4 | async-start | bytes 1376256 | tf_op jit(solution)/shard_map/all_to_all | solution.py:19
  194.1 36.2 %collective-permute-start.2 = (bf16[1120,128]{1,0:T(8,128)(2,1)S(1)}, bf16[1120,128]{1,0:T(8,128)(2,1)S(1)}, u32[]{:S(2)}, u32[]{:S(2)}) collective-permute-start(bf16[1120,128]{1,0:T(8,128)(2,1)S(1)} %get-tuple-element.29), channel_id=1, source_target_pairs={{0,16},{16,0},{32,48},{48,32},{1,17},{17,1},{33,49},{49,33},{2,18}... | collective-permute-start | bytes 860168 | tf_op jit(solution)/shard_map/ppermute | solution.py:47
  196.0 34.3 %collective-permute-start.4 = (bf16[1120,128]{1,0:T(8,128)(2,1)S(1)}, bf16[1120,128]{1,0:T(8,128)(2,1)S(1)}, u32[]{:S(2)}, u32[]{:S(2)}) collective-permute-start(bf16[1120,128]{1,0:T(8,128)(2,1)S(1)} %get-tuple-element.30), channel_id=1, source_target_pairs={{0,48},{16,32},{32,16},{48,0},{1,49},{17,33},{33,17},{49,1},{2,50}... | collective-permute-start | bytes 860168 | tf_op jit(solution)/shard_map/ppermute | solution.py:47
  199.7 30.6 %collective-permute-start.3 = (bf16[1120,128]{1,0:T(8,128)(2,1)S(1)}, bf16[1120,128]{1,0:T(8,128)(2,1)S(1)}, u32[]{:S(2)}, u32[]{:S(2)}) collective-permute-start(bf16[1120,128]{1,0:T(8,128)(2,1)S(1)} %get-tuple-element.31), channel_id=1, source_target_pairs={{0,32},{16,48},{32,0},{48,16},{1,33},{17,49},{33,1},{49,17},{2,34}... | collective-permute-start | bytes 860168 | tf_op jit(solution)/shard_map/ppermute | solution.py:47
  214.6 4.4 %collective-permute-start.5 = (f32[640]{0:T(1024)S(1)}, f32[640]{0:T(1024)S(1)}, u32[]{:S(2)}, u32[]{:S(2)}) collective-permute-start(f32[640]{0:T(1024)S(1)} %convert_reduce_fusion.8), channel_id=1, source_target_pairs={{0,16},{16,0},{32,48},{48,32},{1,17},{17,1},{33,49},{49,33},{2,18}... | collective-permute-start | bytes 7688 | tf_op jit(solution)/shard_map/ppermute | solution.py:47
  218.9 6.5 %collective-permute-start.6 = (f32[640]{0:T(1024)S(1)}, f32[640]{0:T(1024)S(1)}, u32[]{:S(2)}, u32[]{:S(2)}) collective-permute-start(f32[640]{0:T(1024)S(1)} %add.288), channel_id=1, source_target_pairs={{0,32},{16,48},{32,0},{48,16},{1,33},{17,49},{33,1},{49,17},{2,34}... | collective-permute-start | bytes 7688 | tf_op jit(solution)/shard_map/ppermute | solution.py:47
  225.5 4.2 %collective-permute-start.7 = (f32[640]{0:T(1024)S(1)}, f32[640]{0:T(1024)S(1)}, u32[]{:S(2)}, u32[]{:S(2)}) collective-permute-start(f32[640]{0:T(1024)S(1)} %add.289), channel_id=1, source_target_pairs={{0,8},{8,0},{1,9},{9,1},{2,10},{10,2},{3,11},{11,3},{4,12},{12,4},... | collective-permute-start | bytes 7688 | tf_op jit(solution)/shard_map/ppermute | solution.py:47
  230.6 0.7 copy-start.9
  231.2 0.7 copy-start.8
Sparse Core Ops, SparseCore 0:
  43.5 39.3 all-gather.1
